TPU v7x, 32 devices: a whole 2x2x4 slice. The times are simulated.
32 devices in a mesh: dp: 16 (over z, x, core), mp: 2 (over y).
Axes of the slice: x: 2, y: 2, z: 4, core: 2. Of those that a mesh axis runs over, the one named last changes fastest.
Arguments:
- tokens: bfloat16 [64, 512, 768], P('dp', 'mp'), may hold values from -6 to 6
- lengths: int32 [64], P('dp'), may hold values from 128 to 512, as said below
- out_grad: bfloat16 [64, 512, 768], P('dp', 'mp'), may hold values from -6 to 6
- ln1_gain: float32 [768], replicated, may hold values from 0.25 to 1.75
- ln1_shift: float32 [768], replicated, may hold values from -1.75 to 1.75
- w_query: bfloat16 [768, 768], P(None, 'mp'), may hold values from -0.21875 to 0.21875
- b_query: float32 [768], P('mp'), may hold values from -3 to 3
- w_key: bfloat16 [768, 768], P(None, 'mp'), may hold values from -0.21875 to 0.21875
- w_value: bfloat16 [768, 768], P(None, 'mp'), may hold values from -0.21875 to 0.21875
- b_value: float32 [768], P('mp'), may hold values from -3 to 3
- w_out: bfloat16 [768, 768], P('mp'), may hold values from -1.75 to 1.75
- b_out: float32 [768], replicated, may hold values from -1.75 to 1.75
- ln2_gain: float32 [768], replicated, may hold values from 0.25 to 1.75
- ln2_shift: float32 [768], replicated, may hold values from -1.75 to 1.75
- w_up: bfloat16 [768, 3072], P(None, 'mp'), may hold values from -0.21875 to 0.21875
- b_up: float32 [3072], P('mp'), may hold values from -3 to 3
- w_down: bfloat16 [3072, 768], P('mp'), may hold values from -0.109375 to 0.109375
- b_down: float32 [768], replicated, may hold values from -1.75 to 1.75
Outputs:
- block_out: bfloat16 [64, 512, 768], P('dp', 'mp')
- input_grad: float32 [64, 512, 768], P('dp', 'mp')
- grad_ln1_gain: float32 [768], replicated
- grad_ln1_shift: float32 [768], replicated
- grad_w_query: float32 [768, 768], P(None, 'mp')
- grad_b_query: float32 [768], P('mp')
- grad_w_key: float32 [768, 768], P(None, 'mp')
- grad_w_value: float32 [768, 768], P(None, 'mp')
- grad_b_value: float32 [768], P('mp')
- grad_w_out: float32 [768, 768], P('mp')
- grad_b_out: float32 [768], replicated
- grad_ln2_gain: float32 [768], replicated
- grad_ln2_shift: float32 [768], replicated
- grad_w_up: float32 [768, 3072], P(None, 'mp')
- grad_b_up: float32 [3072], P('mp')
- grad_w_down: float32 [3072, 768], P('mp')
- grad_b_down: float32 [768], replicated
Inputs may be any that keep to these rules, and one draw needn't show every extreme that they name: lengths of the rows; some row has 512 and some row a quarter of 512.
All inputs are finite; a program needn't handle non-finite values.
Results may differ from a plain program's by a relative error of at most 0.013.
The roundings to bfloat16 on the way count: a program that leaves them out, or rounds other values in their place, can miss the bound.
Values may be sent and summed in bfloat16 or wider, within the bound.
No kernel may reach another device: no remote copies, remote signals or barrier semaphores. Data moves between devices by JAX's collectives and lax.ppermute only.
A program may use at most 192 MiB of HBM per device.

v0:
```python
import math
import jax
import jax.numpy as jnp
from jax import lax
from jax.sharding import PartitionSpec as P

HEAD_DIM = 64
SEQ = 512
MB = 4
ROWS_MB = 1
epsilon = 1e-12
masked_fill = -1000000000.0


def layer_norm(values, gain_vec, offset):
    average = jnp.mean(values, axis=-1, keepdims=True)
    centred = values - average
    inv_std = lax.rsqrt(jnp.mean(centred * centred, axis=-1, keepdims=True) + epsilon)
    unit_part = centred * inv_std
    return (unit_part * gain_vec + offset, unit_part, inv_std)


def norm_back(upstream, unit_part, inv_std, gain_vec):
    scaled = upstream * gain_vec
    return inv_std * (
        scaled
        - jnp.mean(scaled, axis=-1, keepdims=True)
        - unit_part * jnp.mean(scaled * unit_part, axis=-1, keepdims=True)
    )


def gelu_slope(values):
    normal_cdf = 0.5 * (1.0 + lax.erf(values * (1.0 / math.sqrt(2.0))))
    return normal_cdf + values * jnp.exp(-0.5 * values * values) * (1.0 / math.sqrt(2.0 * math.pi))


def product(pattern, left_side, right_side):
    return jnp.einsum(pattern, left_side, right_side, preferred_element_type=jnp.float32)


def token_sum(values):
    return jnp.sum(values, axis=(0, 1))


def masked_scores(query_low, keys_low, key_valid, score_scale):
    raw_scores = product("bqhd,bkhd->bhqk", query_low, keys_low) * score_scale
    return jnp.where(key_valid, raw_scores, masked_fill)


def on_device(
    tokens,
    lengths,
    out_grad,
    ln1_gain,
    ln1_shift,
    w_query,
    b_query,
    w_key,
    w_value,
    b_value,
    w_out,
    b_out,
    ln2_gain,
    ln2_shift,
    w_up,
    b_up,
    w_down,
    b_down,
):
    heads_here = w_query.shape[1] // HEAD_DIM
    score_scale = 1.0 / math.sqrt(HEAD_DIM)
    positions = jnp.arange(SEQ, dtype=jnp.int32)
    sum_w_query = jnp.zeros(w_query.shape, jnp.float32)
    sum_b_query = jnp.zeros(b_query.shape, jnp.float32)
    sum_w_key = jnp.zeros(w_key.shape, jnp.float32)
    sum_w_value = jnp.zeros(w_value.shape, jnp.float32)
    sum_b_value = jnp.zeros(b_value.shape, jnp.float32)
    sum_w_out = jnp.zeros(w_out.shape, jnp.float32)
    sum_w_up = jnp.zeros(w_up.shape, jnp.float32)
    sum_b_up = jnp.zeros(b_up.shape, jnp.float32)
    sum_w_down = jnp.zeros(w_down.shape, jnp.float32)
    sum_ln1_gain = jnp.zeros(ln1_gain.shape, jnp.float32)
    sum_ln1_shift = jnp.zeros(ln1_shift.shape, jnp.float32)
    sum_ln2_gain = jnp.zeros(ln2_gain.shape, jnp.float32)
    sum_ln2_shift = jnp.zeros(ln2_shift.shape, jnp.float32)
    sum_b_out = jnp.zeros(b_out.shape, jnp.float32)
    sum_b_down = jnp.zeros(b_down.shape, jnp.float32)
    outputs = []
    input_grads = []
    for micro_idx in range(MB):
        row_start = micro_idx * ROWS_MB
        inputs = tokens[row_start : row_start + ROWS_MB].astype(jnp.float32)
        row_lengths = lengths[row_start : row_start + ROWS_MB]
        upstream = out_grad[row_start : row_start + ROWS_MB]
        normed_in, unit_in, inv_in = layer_norm(inputs, ln1_gain, ln1_shift)
        full_in = lax.all_gather(normed_in.astype(jnp.bfloat16), "mp", axis=1, tiled=True)
        rows_mb = full_in.shape[0]
        query_low = (
            (product("bsd,de->bse", full_in, w_query) + b_query)
            .astype(jnp.bfloat16)
            .reshape(rows_mb, SEQ, heads_here, HEAD_DIM)
        )
        keys_low = (
            product("bsd,de->bse", full_in, w_key)
            .astype(jnp.bfloat16)
            .reshape(rows_mb, SEQ, heads_here, HEAD_DIM)
        )
        values_low = (
            (product("bsd,de->bse", full_in, w_value) + b_value)
            .astype(jnp.bfloat16)
            .reshape(rows_mb, SEQ, heads_here, HEAD_DIM)
        )
        key_valid = (positions[None, :] < row_lengths[:, None])[:, None, None, :]
        scores = masked_scores(query_low, keys_low, key_valid, score_scale)
        row_max = jnp.max(scores, axis=-1, keepdims=True)
        log_total = row_max + jnp.log(jnp.sum(jnp.exp(scores - row_max), axis=-1, keepdims=True))
        prob_low = jnp.exp(scores - log_total).astype(jnp.bfloat16)
        mixed_low = (
            product("bhqk,bkhd->bqhd", prob_low, values_low)
            .reshape(rows_mb, SEQ, heads_here * HEAD_DIM)
            .astype(jnp.bfloat16)
        )
        attended = lax.psum_scatter(
            product("bse,ed->bsd", mixed_low, w_out), "mp", scatter_dimension=1, tiled=True
        )
        residual = inputs + attended + b_out
        normed_mid, unit_mid, inv_mid = layer_norm(residual, ln2_gain, ln2_shift)
        full_mid = lax.all_gather(normed_mid.astype(jnp.bfloat16), "mp", axis=1, tiled=True)
        hidden = product("bsd,df->bsf", full_mid, w_up) + b_up
        active = jax.nn.gelu(hidden, approximate=False).astype(jnp.bfloat16)
        branch = lax.psum_scatter(
            product("bsf,fd->bsd", active, w_down).astype(jnp.bfloat16),
            "mp",
            scatter_dimension=1,
            tiled=True,
        ).astype(jnp.float32)
        outputs.append((residual + branch + b_down).astype(jnp.bfloat16))
        grad_full = lax.all_gather(upstream, "mp", axis=1, tiled=True)
        upstream_f = upstream.astype(jnp.float32)
        sum_w_down = sum_w_down + product("bsf,bsd->fd", active, grad_full)
        sum_b_down = sum_b_down + token_sum(upstream_f)
        grad_hidden = (product("bsd,fd->bsf", grad_full, w_down) * gelu_slope(hidden)).astype(
            jnp.bfloat16
        )
        sum_w_up = sum_w_up + product("bsd,bsf->df", full_mid, grad_hidden)
        sum_b_up = sum_b_up + token_sum(grad_hidden.astype(jnp.float32))
        grad_norm_mid = lax.psum_scatter(
            product("bsf,df->bsd", grad_hidden, w_up), "mp", scatter_dimension=1, tiled=True
        )
        sum_ln2_gain = sum_ln2_gain + token_sum(grad_norm_mid * unit_mid)
        sum_ln2_shift = sum_ln2_shift + token_sum(grad_norm_mid)
        grad_residual = upstream_f + norm_back(grad_norm_mid, unit_mid, inv_mid, ln2_gain)
        sum_b_out = sum_b_out + token_sum(grad_residual)
        grad_attn = lax.all_gather(grad_residual.astype(jnp.bfloat16), "mp", axis=1, tiled=True)
        sum_w_out = sum_w_out + product("bse,bsd->ed", mixed_low, grad_attn)
        grad_mixed = (
            product("bsd,ed->bse", grad_attn, w_out)
            .astype(jnp.bfloat16)
            .reshape(rows_mb, SEQ, heads_here, HEAD_DIM)
        )
        grad_probs = product("bqhd,bkhd->bhqk", grad_mixed, values_low)
        probs_full = jnp.exp(masked_scores(query_low, keys_low, key_valid, score_scale) - log_total)
        row_delta = jnp.sum(probs_full * grad_probs, axis=-1, keepdims=True)
        grad_scores = (probs_full * (grad_probs - row_delta)).astype(jnp.bfloat16)
        grad_query = (
            (product("bhqk,bkhd->bqhd", grad_scores, keys_low) * score_scale)
            .astype(jnp.bfloat16)
            .reshape(rows_mb, SEQ, heads_here * HEAD_DIM)
        )
        grad_keys = (
            (product("bhqk,bqhd->bkhd", grad_scores, query_low) * score_scale)
            .astype(jnp.bfloat16)
            .reshape(rows_mb, SEQ, heads_here * HEAD_DIM)
        )
        grad_values = (
            product("bhqk,bqhd->bkhd", prob_low, grad_mixed)
            .astype(jnp.bfloat16)
            .reshape(rows_mb, SEQ, heads_here * HEAD_DIM)
        )
        sum_w_query = sum_w_query + product("bsd,bse->de", full_in, grad_query)
        sum_b_query = sum_b_query + token_sum(grad_query.astype(jnp.float32))
        sum_w_key = sum_w_key + product("bsd,bse->de", full_in, grad_keys)
        sum_w_value = sum_w_value + product("bsd,bse->de", full_in, grad_values)
        sum_b_value = sum_b_value + token_sum(grad_values.astype(jnp.float32))
        input_terms = (
            product("bse,de->bsd", grad_query, w_query)
            + product("bse,de->bsd", grad_keys, w_key)
            + product("bse,de->bsd", grad_values, w_value)
        )
        grad_norm_in = lax.psum_scatter(
            input_terms.astype(jnp.bfloat16), "mp", scatter_dimension=1, tiled=True
        ).astype(jnp.float32)
        sum_ln1_gain = sum_ln1_gain + token_sum(grad_norm_in * unit_in)
        sum_ln1_shift = sum_ln1_shift + token_sum(grad_norm_in)
        input_grads.append(grad_residual + norm_back(grad_norm_in, unit_in, inv_in, ln1_gain))
    totals = tuple(
        lax.psum(
            (
                sum_w_query,
                sum_b_query,
                sum_w_key,
                sum_w_value,
                sum_b_value,
                sum_w_out,
                sum_w_up,
                sum_b_up,
                sum_w_down,
            ),
            "dp",
        )
    )
    common = lax.psum(
        (sum_ln1_gain, sum_ln1_shift, sum_ln2_gain, sum_ln2_shift, sum_b_out, sum_b_down),
        ("dp", "mp"),
    )
    block_out = jnp.concatenate(outputs, axis=0)
    input_grad = jnp.concatenate(input_grads, axis=0)
    return (
        block_out,
        input_grad,
        common[0],
        common[1],
        totals[0],
        totals[1],
        totals[2],
        totals[3],
        totals[4],
        totals[5],
        common[4],
        common[2],
        common[3],
        totals[6],
        totals[7],
        totals[8],
        common[5],
    )


def solution(mesh):
    in_specs = (
        P("dp", "mp", None),
        P("dp"),
        P("dp", "mp", None),
        P(),
        P(),
        P(None, "mp"),
        P("mp"),
        P(None, "mp"),
        P(None, "mp"),
        P("mp"),
        P("mp", None),
        P(),
        P(),
        P(),
        P(None, "mp"),
        P("mp"),
        P("mp", None),
        P(),
    )
    out_specs = (
        P("dp", "mp", None),
        P("dp", "mp", None),
        P(),
        P(),
        P(None, "mp"),
        P("mp"),
        P(None, "mp"),
        P(None, "mp"),
        P("mp"),
        P("mp", None),
        P(),
        P(),
        P(),
        P(None, "mp"),
        P("mp"),
        P("mp", None),
        P(),
    )
    return jax.shard_map(
        on_device, mesh=mesh, in_specs=in_specs, out_specs=out_specs, check_vma=False
    )
```

profile of v0, /device:TPU:0, one launch (start us, length us, event | category | flops | bytes accessed | tf_op | source)
XLA Modules:
  0.0 932.4 jit_solution(8912068039627414131)
XLA Ops:
  12.2 12.8 %all_gather.52 = bf16[1,512,768]{2,1,0:T(8,128)(2,1)S(1)} all-gather(bf16[1,256,768]{2,1,0:T(8,128)(2,1)S(1)} %fusion.127), channel_id=1, replica_groups=mesh['dp'=16,'mp'=2] {'mp'}, dimensions={1}, use_global_device_ids=true | all-gather | bytes 1179648 | tf_op jit(solution)/shard_map/all_gather | solution.py:96
  40.5 16.8 %all_gather.60 = bf16[1,512,768]{2,1,0:T(8,128)(2,1)} all-gather(bf16[1,256,768]{2,1,0:T(8,128)(2,1)S(1)} %get-tuple-element.113), channel_id=1, replica_groups=mesh['dp'=16,'mp'=2] {'mp'}, dimensions={1}, use_global_device_ids=true | all-gather | bytes 1179648 | tf_op jit(solution)/shard_map/all_gather | solution.py:138
  57.3 12.3 %reduce-scatter.25.cloned.1.call-done = f32[1,256,768]{2,1,0:T(8,128)} async-done(((f32[1,512,768]{2,1,0:T(8,128)}), f32[1,256,768]{2,1,0:T(8,128)}) %reduce-scatter.25.cloned.1.call-update) | async-done | bytes 786448 | tf_op jit(solution)/shard_map/reduce_scatter | solution.py:123
  72.2 12.0 %all_gather.53 = bf16[1,512,768]{2,1,0:T(8,128)(2,1)S(1)} all-gather(bf16[1,256,768]{2,1,0:T(8,128)(2,1)S(1)} %add_convert_fusion.7), channel_id=1, replica_groups=mesh['dp'=16,'mp'=2] {'mp'}, dimensions={1}, use_global_device_ids=true | all-gather | bytes 1179648 | tf_op jit(solution)/shard_map/all_gather | solution.py:128
  84.2 10.3 %fusion.16 = (bf16[512,1536]{1,0:T(8,128)(2,1)}, f32[512,1536]{1,0:T(8,128)S(1)}) fusion(f32[1536]{0:T(1024)} %param.33, bf16[768,1536]{1,0:T(8,128)(2,1)S(1)} %copy-done, bf16[1,512,768]{2,1,0:T(8,128)(2,1)S(1)} %all_gather.53), kind=kOutput, calls=%fused_computation.54 | convolution fusion | flops 1259864064 | bytes 7870464 | tf_op jit(solution)/shard_map/bsd,df->bsf/dot_general | solution.py:38
  105.7 22.8 %reduce-scatter.41.cloned.1.call-done = f32[1,256,768]{2,1,0:T(8,128)} async-done(((f32[1,512,768]{2,1,0:T(8,128)}), f32[1,256,768]{2,1,0:T(8,128)}) %reduce-scatter.41.cloned.1.call-update) | async-done | bytes 786448 | tf_op jit(solution)/shard_map/reduce_scatter | solution.py:147
  131.2 17.6 %reduce-scatter.27.cloned.1.call-done = bf16[1,256,768]{2,1,0:T(8,128)(2,1)} async-done(((bf16[1,512,768]{2,1,0:T(8,128)(2,1)}), bf16[1,256,768]{2,1,0:T(8,128)(2,1)}) %reduce-scatter.27.cloned.1.call-update) | async-done | bytes 393232 | tf_op jit(solution)/shard_map/reduce_scatter | solution.py:131
  152.5 12.1 %all_gather.61 = bf16[1,512,768]{2,1,0:T(8,128)(2,1)S(1)} all-gather(bf16[1,256,768]{2,1,0:T(8,128)(2,1)S(1)} %convert_element_type.620), channel_id=1, replica_groups=mesh['dp'=16,'mp'=2] {'mp'}, dimensions={1}, use_global_device_ids=true | all-gather | bytes 1179648 | tf_op jit(solution)/shard_map/all_gather | solution.py:154
  181.2 15.7 %reduce-scatter.43.cloned.1.call-done = bf16[1,256,768]{2,1,0:T(8,128)(2,1)} async-done(((bf16[1,512,768]{2,1,0:T(8,128)(2,1)}), bf16[1,256,768]{2,1,0:T(8,128)(2,1)}) %reduce-scatter.43.cloned.1.call-update) | async-done | bytes 393232 | tf_op jit(solution)/shard_map/reduce_scatter | solution.py:190
  202.5 11.8 %all_gather.54 = bf16[1,512,768]{2,1,0:T(8,128)(2,1)S(1)} all-gather(bf16[1,256,768]{2,1,0:T(8,128)(2,1)S(1)} %get-tuple-element.97), channel_id=1, replica_groups=mesh['dp'=16,'mp'=2] {'mp'}, dimensions={1}, use_global_device_ids=true | all-gather | bytes 1179648 | tf_op jit(solution)/shard_map/all_gather | solution.py:96
  228.0 16.7 %all_gather.50 = bf16[1,512,768]{2,1,0:T(8,128)(2,1)S(1)} all-gather(bf16[1,256,768]{2,1,0:T(8,128)(2,1)} %get-tuple-element.96), channel_id=1, replica_groups=mesh['dp'=16,'mp'=2] {'mp'}, dimensions={1}, use_global_device_ids=true | all-gather | bytes 1179648 | tf_op jit(solution)/shard_map/all_gather | solution.py:96
  259.6 9.8 %all_gather.48 = bf16[1,512,768]{2,1,0:T(8,128)(2,1)S(1)} all-gather(bf16[1,256,768]{2,1,0:T(8,128)(2,1)} %get-tuple-element.95), channel_id=1, replica_groups=mesh['dp'=16,'mp'=2] {'mp'}, dimensions={1}, use_global_device_ids=true | all-gather | bytes 1179648 | tf_op jit(solution)/shard_map/all_gather | solution.py:96
  283.6 10.3 %all_gather.62 = bf16[1,512,768]{2,1,0:T(8,128)(2,1)} all-gather(bf16[1,256,768]{2,1,0:T(8,128)(2,1)} %get-tuple-element.112), channel_id=1, replica_groups=mesh['dp'=16,'mp'=2] {'mp'}, dimensions={1}, use_global_device_ids=true | all-gather | bytes 1179648 | tf_op jit(solution)/shard_map/all_gather | solution.py:138
  293.9 17.9 %all_gather.58 = bf16[1,512,768]{2,1,0:T(8,128)(2,1)} all-gather(bf16[1,256,768]{2,1,0:T(8,128)(2,1)} %get-tuple-element.111), channel_id=1, replica_groups=mesh['dp'=16,'mp'=2] {'mp'}, dimensions={1}, use_global_device_ids=true | all-gather | bytes 1179648 | tf_op jit(solution)/shard_map/all_gather | solution.py:138
  311.8 16.6 %all_gather.56 = bf16[1,512,768]{2,1,0:T(8,128)(2,1)} all-gather(bf16[1,256,768]{2,1,0:T(8,128)(2,1)S(1)} %copy-done.115), channel_id=1, replica_groups=mesh['dp'=16,'mp'=2] {'mp'}, dimensions={1}, use_global_device_ids=true | all-gather | bytes 1179648 | tf_op jit(solution)/shard_map/all_gather | solution.py:138
  332.8 11.8 %all_gather.55 = bf16[1,512,768]{2,1,0:T(8,128)(2,1)} all-gather(bf16[1,256,768]{2,1,0:T(8,128)(2,1)S(1)} %get-tuple-element.120), channel_id=1, replica_groups=mesh['dp'=16,'mp'=2] {'mp'}, dimensions={1}, use_global_device_ids=true | all-gather | bytes 1179648 | tf_op jit(solution)/shard_map/all_gather | solution.py:128
  344.7 10.9 %all_gather.51 = bf16[1,512,768]{2,1,0:T(8,128)(2,1)S(1)} all-gather(bf16[1,256,768]{2,1,0:T(8,128)(2,1)S(1)} %get-tuple-element.119), channel_id=1, replica_groups=mesh['dp'=16,'mp'=2] {'mp'}, dimensions={1}, use_global_device_ids=true | all-gather | bytes 1179648 | tf_op jit(solution)/shard_map/all_gather | solution.py:128
  355.6 9.4 %fusion.13 = (bf16[512,1536]{1,0:T(8,128)(2,1)}, f32[512,1536]{1,0:T(8,128)S(1)}) fusion(f32[1536]{0:T(1024)S(1)} %copy-done.189, bf16[768,1536]{1,0:T(8,128)(2,1)S(1)} %copy-done, bf16[1,512,768]{2,1,0:T(8,128)(2,1)S(1)} %all_gather.51), kind=kOutput, calls=%fused_computation.51 | convolution fusion | flops 1259864064 | bytes 7870464 | tf_op jit(solution)/shard_map/bsd,df->bsf/dot_general | solution.py:38
  365.0 10.5 %all_gather.49 = bf16[1,512,768]{2,1,0:T(8,128)(2,1)} all-gather(bf16[1,256,768]{2,1,0:T(8,128)(2,1)S(1)} %get-tuple-element.118), channel_id=1, replica_groups=mesh['dp'=16,'mp'=2] {'mp'}, dimensions={1}, use_global_device_ids=true | all-gather | bytes 1179648 | tf_op jit(solution)/shard_map/all_gather | solution.py:128
  382.2 9.8 %fusion.19 = (bf16[512,1536]{1,0:T(8,128)(2,1)}, f32[512,1536]{1,0:T(8,128)S(1)}) fusion(f32[1536]{0:T(1024)S(1)} %copy-done.189, bf16[768,1536]{1,0:T(8,128)(2,1)S(1)} %copy-done, bf16[1,512,768]{2,1,0:T(8,128)(2,1)} %all_gather.55), kind=kOutput, calls=%fused_computation.57 | convolution fusion | flops 1259864064 | bytes 7870464 | tf_op jit(solution)/shard_map/bsd,df->bsf/dot_general | solution.py:38
  398.9 9.8 %fusion.10 = (bf16[512,1536]{1,0:T(8,128)(2,1)}, f32[512,1536]{1,0:T(8,128)S(1)}) fusion(f32[1536]{0:T(1024)S(1)} %copy-done.189, bf16[768,1536]{1,0:T(8,128)(2,1)S(1)} %copy-done, bf16[1,512,768]{2,1,0:T(8,128)(2,1)} %all_gather.49), kind=kOutput, calls=%fused_computation.48 | convolution fusion | flops 1259864064 | bytes 7870464 | tf_op jit(solution)/shard_map/bsd,df->bsf/dot_general | solution.py:38
  420.0 5.4 fusion.162
  450.2 9.8 %add_add_fusion = f32[1536,768]{1,0:T(8,128)} fusion(f32[1536,768]{1,0:T(8,128)} %fusion.162, f32[1536,768]{1,0:T(8,128)} %fusion.173, f32[1536,768]{1,0:T(8,128)} %fusion.167, bf16[512,1536]{1,0:T(8,128)(2,1)} %get-tuple-element.145, bf16[1,512,768]{2,1,0:T(8,128)(2,1)} %all_gather.62), kind=kOutput, calls=%fused_computation.32 | convolution fusion | flops 1211498496 | bytes 21233664 | tf_op jit(solution)/shard_map/bsf,bsd->fd/dot_general | solution.py:38
  460.0 9.1 add_add_fusion.1
  472.8 13.2 %reduce-scatter.19.cloned.1.call-done = bf16[1,256,768]{2,1,0:T(8,128)(2,1)} async-done(((bf16[1,512,768]{2,1,0:T(8,128)(2,1)}), bf16[1,256,768]{2,1,0:T(8,128)(2,1)}) %reduce-scatter.19.cloned.1.call-update) | async-done | bytes 393232 | tf_op jit(solution)/shard_map/reduce_scatter | solution.py:131
  486.1 20.2 %reduce-scatter.31.cloned.1.call-done = bf16[1,256,768]{2,1,0:T(8,128)(2,1)} async-done(((bf16[1,512,768]{2,1,0:T(8,128)(2,1)}), bf16[1,256,768]{2,1,0:T(8,128)(2,1)}) %reduce-scatter.31.cloned.1.call-update) | async-done | bytes 393232 | tf_op jit(solution)/shard_map/reduce_scatter | solution.py:131
  511.3 19.5 %all_gather.57 = bf16[1,512,768]{2,1,0:T(8,128)(2,1)S(1)} all-gather(bf16[1,256,768]{2,1,0:T(8,128)(2,1)S(1)} %convert_element_type.586), channel_id=1, replica_groups=mesh['dp'=16,'mp'=2] {'mp'}, dimensions={1}, use_global_device_ids=true | all-gather | bytes 1179648 | tf_op jit(solution)/shard_map/all_gather | solution.py:154
  547.8 8.5 all_gather.59
  568.1 8.6 all_gather.63
  642.5 60.4 %all-reduce.1 = (f32[384]{0:T(512)}, f32[384]{0:T(512)}, f32[1536]{0:T(1024)}) all-reduce(f32[384]{0:T(512)} %add.700, f32[384]{0:T(512)} %add.710, f32[1536]{0:T(1024)S(1)} %add_add_fusion.2), channel_id=1, replica_groups=mesh['dp'=16,'mp'=2] {'dp'}, use_global_device_ids=true, to_apply=%region_75.76 | all-reduce | flops 2304 | bytes 18432 | tf_op jit(solution)/shard_map/psum | solution.py:197
  713.4 39.4 %all-reduce = (f32[768]{0:T(1024)}, f32[768]{0:T(1024)}, f32[768]{0:T(1024)}, f32[768]{0:T(1024)}, f32[768]{0:T(1024)}, /*index=5*/f32[768]{0:T(1024)}) all-reduce(f32[768]{0:T(1024)} %add_add_fusion.10, f32[768]{0:T(1024)} %add_add_fusion.9, f32[768]{0:T(1024)} %add_add_fusion.6, ...), channel_id=1, replica_groups=mesh['dp'=16,'mp'=2] {'dp','mp'}, use_global_device_ids=true, to_apply=%region_64.65 | all-reduce | flops 4608 | bytes 36864 | tf_op jit(solution)/shard_map/psum | solution.py:212
  763.1 151.8 %all-reduce.5.cloned.1.call-done = (f32[768,384]{1,0:T(8,128)}, f32[768,384]{1,0:T(8,128)}, f32[768,384]{1,0:T(8,128)}, f32[384,768]{1,0:T(8,128)}, f32[768,1536]{1,0:T(8,128)}, /*index=5*/f32[1536,768]{1,0:T(8,128)}) async-done(((f32[768,384]{1,0:T(8,128)}, f32[768,384]{1,0:T(8,128)}, f32[768,384]{1,0:T(8,128)}, f32[384,768]{1,0:T(8,128)}, f32[768,1536]{1,0:T(8,128)}, /*index=5*/f32[1536,768]{1,0:T(8,128)}), ...) | async-done | bytes 14155792 | tf_op jit(solution)/shard_map/psum | solution.py:197
  (646 shorter events, 292.1 us)
Async XLA Ops:
  7.2 77.0 %copy-start = (bf16[768,1536]{1,0:T(8,128)(2,1)S(1)}, bf16[768,1536]{1,0:T(8,128)(2,1)}, u32[]{:S(2)}) copy-start(bf16[768,1536]{1,0:T(8,128)(2,1)} %param.32) | copy-start | bytes 7077892
  7.2 62.3 %reduce-scatter.25.cloned.1.call-start = ((), (), s32[]{:S(2)}) async-start(), calls=%async_computation.20 | async-start | bytes 2359296 | tf_op jit(solution)/shard_map/reduce_scatter | solution.py:123
  38.0 90.5 %reduce-scatter.41.cloned.1.call-start = ((), (), s32[]{:S(2)}) async-start(), calls=%async_computation.28 | async-start | bytes 2359296 | tf_op jit(solution)/shard_map/reduce_scatter | solution.py:147
  101.1 47.7 %reduce-scatter.27.cloned.1.call-start = ((), (), s32[]{:S(2)}) async-start(), calls=%async_computation.21 | async-start | bytes 1179648 | tf_op jit(solution)/shard_map/reduce_scatter | solution.py:131
  105.6 91.3 %reduce-scatter.43.cloned.1.call-start = ((), (), s32[]{:S(2)}) async-start(), calls=%async_computation.29 | async-start | bytes 1179648 | tf_op jit(solution)/shard_map/reduce_scatter | solution.py:190
  179.3 149.1 %reduce-scatter.29.cloned.1.call-start = ((), (), s32[]{:S(2)}) async-start(), calls=%async_computation.22 | async-start | bytes 2359296 | tf_op jit(solution)/shard_map/reduce_scatter | solution.py:123
  180.5 35.0 %copy-start.144 = (f32[256]{0:T(256)}, f32[256]{0:T(256)S(1)}, u32[]{:S(2)}) copy-start(f32[256]{0:T(256)S(1)} %broadcast_multiply_fusion.17) | copy-start | bytes 3076
  181.2 34.4 %copy-start.148 = (f32[256]{0:T(256)}, f32[256]{0:T(256)S(1)}, u32[]{:S(2)}) copy-start(f32[256]{0:T(256)S(1)} %get-tuple-element.182) | copy-start | bytes 3076
  227.3 101.2 %reduce-scatter.21.cloned.1.call-start = ((), (), s32[]{:S(2)}) async-start(), calls=%async_computation.18 | async-start | bytes 2359296 | tf_op jit(solution)/shard_map/reduce_scatter | solution.py:123
  258.8 70.4 %reduce-scatter.17.cloned.1.call-start = ((), (), s32[]{:S(2)}) async-start(), calls=%async_computation.16 | async-start | bytes 2359296 | tf_op jit(solution)/shard_map/reduce_scatter | solution.py:123
  283.5 45.7 %copy-start.166 = (f32[768]{0:T(1024)S(1)}, f32[768]{0:T(1024)}, u32[]{:S(2)}) copy-start(f32[768]{0:T(1024)} %param.29) | copy-start | bytes 9220
  283.5 185.6 %reduce-scatter.37.cloned.1.call-start = ((), (), s32[]{:S(2)}) async-start(), calls=%async_computation.26 | async-start | bytes 2359296 | tf_op jit(solution)/shard_map/reduce_scatter | solution.py:147
  331.8 137.2 %copy-start.146 = (f32[256]{0:T(256)}, f32[256]{0:T(256)S(1)}, u32[]{:S(2)}) copy-start(f32[256]{0:T(256)S(1)} %broadcast_multiply_fusion.20) | copy-start | bytes 3076
  332.1 137.0 %copy-start.172 = (f32[256]{0:T(256)}, f32[256]{0:T(256)S(1)}, u32[]{:S(2)}) copy-start(f32[256]{0:T(256)S(1)} %add_rsqrt_fusion.4) | copy-start | bytes 3076
  382.1 87.0 %reduce-scatter.45.cloned.1.call-start = ((), (), s32[]{:S(2)}) async-start(), calls=%async_computation.30 | async-start | bytes 2359296 | tf_op jit(solution)/shard_map/reduce_scatter | solution.py:147
  398.6 70.4 %reduce-scatter.33.cloned.1.call-start = ((), (), s32[]{:S(2)}) async-start(), calls=%async_computation.24 | async-start | bytes 2359296 | tf_op jit(solution)/shard_map/reduce_scatter | solution.py:147
  415.3 70.8 %reduce-scatter.19.cloned.1.call-start = ((), (), s32[]{:S(2)}) async-start(), calls=%async_computation.17 | async-start | bytes 1179648 | tf_op jit(solution)/shard_map/reduce_scatter | solution.py:131
  419.9 86.4 %reduce-scatter.31.cloned.1.call-start = ((), (), s32[]{:S(2)}) async-start(), calls=%async_computation.23 | async-start | bytes 1179648 | tf_op jit(solution)/shard_map/reduce_scatter | solution.py:131
  434.9 109.7 %reduce-scatter.23.cloned.1.call-start = ((), (), s32[]{:S(2)}) async-start(), calls=%async_computation.19 | async-start | bytes 1179648 | tf_op jit(solution)/shard_map/reduce_scatter | solution.py:131
  450.2 257.0 %reduce-scatter.35.cloned.1.call-start = ((), (), s32[]{:S(2)}) async-start(), calls=%async_computation.25 | async-start | bytes 1179648 | tf_op jit(solution)/shard_map/reduce_scatter | solution.py:190
  469.1 37.2 %copy-start.142 = (f32[768]{0:T(1024)S(1)}, f32[768]{0:T(1024)}, u32[]{:S(2)}) copy-start(f32[768]{0:T(1024)} %param.35) | copy-start | bytes 9220
  588.7 118.5 %reduce-scatter.39.cloned.1.call-start = ((), (), s32[]{:S(2)}) async-start(), calls=%async_computation.27 | async-start | bytes 1179648 | tf_op jit(solution)/shard_map/reduce_scatter | solution.py:190
  609.2 98.0 %reduce-scatter.47.cloned.1.call-start = ((), (), s32[]{:S(2)}) async-start(), calls=%async_computation.31 | async-start | bytes 1179648 | tf_op jit(solution)/shard_map/reduce_scatter | solution.py:190
  623.6 291.2 %all-reduce.5.cloned.1.call-start = ((), (), s32[]{:S(2)}) async-start(), calls=%async_computation.32 | async-start | bytes 28311552 | tf_op jit(solution)/shard_map/psum | solution.py:197
  632.0 71.0 %copy-start.105 = (bf16[1,256,768]{2,1,0:T(8,128)(2,1)S(1)}, bf16[1,256,768]{2,1,0:T(8,128)(2,1)}, u32[]{:S(2)}) copy-start(bf16[1,256,768]{2,1,0:T(8,128)(2,1)} %get-tuple-element.114) | copy-start | bytes 1179652
  632.0 71.0 %copy-start.112 = (bf16[1,256,768]{2,1,0:T(8,128)(2,1)S(1)}, bf16[1,256,768]{2,1,0:T(8,128)(2,1)}, u32[]{:S(2)}) copy-start(bf16[1,256,768]{2,1,0:T(8,128)(2,1)} %get-tuple-element.117) | copy-start | bytes 1179652
  632.0 71.0 %copy-start.116 = (bf16[1,256,768]{2,1,0:T(8,128)(2,1)S(1)}, bf16[1,256,768]{2,1,0:T(8,128)(2,1)}, u32[]{:S(2)}) copy-start(bf16[1,256,768]{2,1,0:T(8,128)(2,1)} %get-tuple-element.115) | copy-start | bytes 1179652
  632.0 75.2 %copy-start.141 = (f32[768]{0:T(1024)S(1)}, f32[768]{0:T(1024)}, u32[]{:S(2)}) copy-start(f32[768]{0:T(1024)} %param.21) | copy-start | bytes 9220
  632.0 75.2 %copy-start.145 = (f32[256]{0:T(256)S(1)}, f32[256]{0:T(256)}, u32[]{:S(2)}) copy-start(f32[256]{0:T(256)} %copy-done.144) | copy-start | bytes 3076
  707.2 52.6 %copy-start.44 = (f32[1,256,768]{2,1,0:T(8,128)S(1)}, f32[1,256,768]{2,1,0:T(8,128)}, u32[]{:S(2)}) copy-start(f32[1,256,768]{2,1,0:T(8,128)} %copy-done.43) | copy-start | bytes 2359300
  707.2 52.7 %copy-start.150 = (f32[256]{0:T(256)S(1)}, f32[256]{0:T(256)}, u32[]{:S(2)}) copy-start(f32[256]{0:T(256)} %copy-done.149) | copy-start | bytes 3076
  707.2 52.6 %copy-start.117 = (bf16[1,256,768]{2,1,0:T(8,128)(2,1)S(1)}, bf16[1,256,768]{2,1,0:T(8,128)(2,1)}, u32[]{:S(2)}) copy-start(bf16[1,256,768]{2,1,0:T(8,128)(2,1)} %reduce-scatter.47.cloned.1.call-done) | copy-start | bytes 1179652
  (191 other events, 1234.1 us)
Sparse Core Ops, SparseCore 0:
  38.1 31.3 reduce-scatter.24
  101.3 27.2 reduce-scatter.40
  131.3 17.4 reduce-scatter.26
  179.4 17.4 reduce-scatter.42
  227.4 29.7 reduce-scatter.28
  260.0 29.1 reduce-scatter.20
  292.0 37.1 reduce-scatter.16
  382.2 26.8 reduce-scatter.36
  411.4 26.0 reduce-scatter.44
  439.7 26.0 reduce-scatter.32
  468.6 17.4 reduce-scatter.18
  488.8 17.4 reduce-scatter.30
  509.1 23.6 reduce-scatter.22
  588.8 17.3 reduce-scatter.34
  609.3 17.3 reduce-scatter.38
  629.5 17.4 reduce-scatter.46
  653.1 261.7 all-reduce.4
where the time goes:
time: 940 us; the launch traced here: 932 us
  blocking collectives  307 us (33%)
  waiting for transfers between devices  255 us (27%)
  matrix products  229 us (24%)
  other arithmetic  87.3 us (9%)
  local copies, waits for them, and re-layouts  37.1 us (4%)
  between operations  16.6 us (2%)
    dot_general x96, matrix products, product(): jnp.einsum(pattern, left_side, right_side, preferred_element_type=jnp.flo...  229 us
    psum x1, waiting for transfers between devices, on_device(): lax.psum((sum_w_query, sum_b_query, sum_w_key, sum_w_value, sum_b_value,...  152 us
    all_gather x4, blocking collectives, on_device(): grad_full = lax.all_gather(upstream, 'mp', axis=1, tiled=True)  61.7 us
    psum x1, blocking collectives, on_device(): lax.psum((sum_w_query, sum_b_query, sum_w_key, sum_w_value, sum_b_value,...  60.4 us
    all_gather x4, blocking collectives, on_device(): lax.all_gather(normed_in.astype(jnp.bfloat16), 'mp', axis=1, tiled=True)  51.1 us
    reduce_scatter x4, waiting for transfers between devices, on_device(): lax.psum_scatter(product('bsf,fd->bsd', active, w_down).astype(jnp.bfloat...  51 us
    all_gather x4, blocking collectives, on_device(): lax.all_gather(grad_residual.astype(jnp.bfloat16), 'mp', axis=1, tiled=True)  48.7 us
    all_gather x4, blocking collectives, on_device(): lax.all_gather(normed_mid.astype(jnp.bfloat16), 'mp', axis=1, tiled=True)  45.3 us
  transfers between devices with their start and end apart: 17, of which 8 were waited for; matrix products, arithmetic and copies ran while one was open for 23% of the time, Pallas kernels for 0%

commit v1 on v0

--- a/solution.py
+++ b/solution.py
@@ -10,6 +10,22 @@
 ROWS_MB = 1
 epsilon = 1e-12
 masked_fill = -1000000000.0
+
+
+def shifts_all_set(u_in):
+    left_arr, everything, finding = (lax.axis_size("mp"), lax.axis_index("mp"), u_in.shape[1])
+    front, o_now = (u_in, 1)
+    while o_now < left_arr:
+        front = jnp.concatenate(
+            [
+                front,
+                lax.ppermute(front, "mp", [(d, (d - o_now) % left_arr) for d in range(left_arr)]),
+            ],
+            axis=1,
+        )
+        o_now = 2 * o_now
+    q_next = jnp.roll(front, everything * finding, axis=1)
+    return q_next
 
 
 def layer_norm(values, gain_vec, offset):
@@ -93,7 +109,7 @@
         row_lengths = lengths[row_start : row_start + ROWS_MB]
         upstream = out_grad[row_start : row_start + ROWS_MB]
         normed_in, unit_in, inv_in = layer_norm(inputs, ln1_gain, ln1_shift)
-        full_in = lax.all_gather(normed_in.astype(jnp.bfloat16), "mp", axis=1, tiled=True)
+        full_in = shifts_all_set(normed_in.astype(jnp.bfloat16))
         rows_mb = full_in.shape[0]
         query_low = (
             (product("bsd,de->bse", full_in, w_query) + b_query)

time: 940 us -> 940 us (level)
  blocking collectives: 307 us -> 256 us
  waiting for transfers between devices: 255 us -> 291 us
    all_gather x4 -> x0, blocking collectives: 51.1 us -> none  [on_device(): lax.all_gather(normed_in.astype(jnp.bfloat16), 'mp', axis=1, tiled=True)]
    reduce_scatter x4, waiting for transfers between devices: 13 us -> 31.7 us  [on_device(): lax.psum_scatter(product('bse,ed->bsd', mixed_low, w_out), 'mp', scatter_...]
    ppermute x0 -> x4, waiting for transfers between devices: none -> 16.6 us  [shifts_all_set(): lax.ppermute(front, 'mp', [(d, (d - o_now) % left_arr) for d in range(lef...]
    unnamed x418 -> x434, local copies, waits for them, and re-layouts: 31.2 us -> 30.2 us
  transfers between devices with their start and end apart: 17 -> 21, of which waited for: 8 -> 10; matrix products, arithmetic and copies ran while one was open for 23% -> 24% of each run, Pallas kernels for 0% -> 0%
where the time goes in v1:
time: 940 us; the launch traced here: 932 us
  waiting for transfers between devices  291 us (31%)
  blocking collectives  256 us (27%)
  matrix products  228 us (24%)
  other arithmetic  96 us (10%)
  local copies, waits for them, and re-layouts  36.7 us (4%)
  between operations  16.8 us (2%)
    dot_general x96, matrix products, product(): jnp.einsum(pattern, left_side, right_side, preferred_element_type=jnp.flo...  228 us
    psum x1, waiting for transfers between devices, on_device(): lax.psum((sum_w_query, sum_b_query, sum_w_key, sum_w_value, sum_b_value,...  153 us
    all_gather x4, blocking collectives, on_device(): grad_full = lax.all_gather(upstream, 'mp', axis=1, tiled=True)  63.8 us
    psum x1, blocking collectives, on_device(): lax.psum((sum_w_query, sum_b_query, sum_w_key, sum_w_value, sum_b_value,...  60.3 us
    reduce_scatter x4, waiting for transfers between devices, on_device(): lax.psum_scatter(product('bsf,fd->bsd', active, w_down).astype(jnp.bfloat...  49.8 us
    all_gather x4, blocking collectives, on_device(): lax.all_gather(grad_residual.astype(jnp.bfloat16), 'mp', axis=1, tiled=True)  48.4 us
    all_gather x4, blocking collectives, on_device(): lax.all_gather(normed_mid.astype(jnp.bfloat16), 'mp', axis=1, tiled=True)  44.2 us
    psum x1, blocking collectives, on_device(): lax.psum((sum_ln1_gain, sum_ln1_shift, sum_ln2_gain, sum_ln2_shift, sum_b...  39.3 us
  transfers between devices with their start and end apart: 21, of which 10 were waited for; matrix products, arithmetic and copies ran while one was open for 24% of the time, Pallas kernels for 0%

profile of v1, /device:TPU:0, one launch (start us, length us, event | category | flops | bytes accessed | tf_op | source)
XLA Modules:
  0.0 931.9 jit_solution(13502382230643735918)
XLA Ops:
  18.0 7.3 collective-permute-done.2
  41.4 16.8 %all_gather.44 = bf16[1,512,768]{2,1,0:T(8,128)(2,1)} all-gather(bf16[1,256,768]{2,1,0:T(8,128)(2,1)S(1)} %get-tuple-element.114), channel_id=1, replica_groups=mesh['dp'=16,'mp'=2] {'mp'}, dimensions={1}, use_global_device_ids=true | all-gather | bytes 1179648 | tf_op jit(solution)/shard_map/all_gather | solution.py:154
  58.2 12.3 %reduce-scatter.25.cloned.1.call-done = f32[1,256,768]{2,1,0:T(8,128)} async-done(((f32[1,512,768]{2,1,0:T(8,128)}), f32[1,256,768]{2,1,0:T(8,128)}) %reduce-scatter.25.cloned.1.call-update) | async-done | bytes 786448 | tf_op jit(solution)/shard_map/reduce_scatter | solution.py:139
  73.1 11.9 %all_gather.38 = bf16[1,512,768]{2,1,0:T(8,128)(2,1)S(1)} all-gather(bf16[1,256,768]{2,1,0:T(8,128)(2,1)S(1)} %add_convert_fusion.7), channel_id=1, replica_groups=mesh['dp'=16,'mp'=2] {'mp'}, dimensions={1}, use_global_device_ids=true | all-gather | bytes 1179648 | tf_op jit(solution)/shard_map/all_gather | solution.py:144
  85.1 10.3 %fusion.16 = (bf16[512,1536]{1,0:T(8,128)(2,1)}, f32[512,1536]{1,0:T(8,128)S(1)}) fusion(f32[1536]{0:T(1024)} %param.35, bf16[768,1536]{1,0:T(8,128)(2,1)S(1)} %copy-done, bf16[1,512,768]{2,1,0:T(8,128)(2,1)S(1)} %all_gather.38), kind=kOutput, calls=%fused_computation.54 | convolution fusion | flops 1259864064 | bytes 7870464 | tf_op jit(solution)/shard_map/bsd,df->bsf/dot_general | solution.py:54
  106.4 22.8 %reduce-scatter.41.cloned.1.call-done = f32[1,256,768]{2,1,0:T(8,128)} async-done(((f32[1,512,768]{2,1,0:T(8,128)}), f32[1,256,768]{2,1,0:T(8,128)}) %reduce-scatter.41.cloned.1.call-update) | async-done | bytes 786448 | tf_op jit(solution)/shard_map/reduce_scatter | solution.py:163
  132.0 17.6 %reduce-scatter.27.cloned.1.call-done = bf16[1,256,768]{2,1,0:T(8,128)(2,1)} async-done(((bf16[1,512,768]{2,1,0:T(8,128)(2,1)}), bf16[1,256,768]{2,1,0:T(8,128)(2,1)}) %reduce-scatter.27.cloned.1.call-update) | async-done | bytes 393232 | tf_op jit(solution)/shard_map/reduce_scatter | solution.py:147
  153.2 11.5 %all_gather.45 = bf16[1,512,768]{2,1,0:T(8,128)(2,1)S(1)} all-gather(bf16[1,256,768]{2,1,0:T(8,128)(2,1)S(1)} %convert_element_type.620), channel_id=1, replica_groups=mesh['dp'=16,'mp'=2] {'mp'}, dimensions={1}, use_global_device_ids=true | all-gather | bytes 1179648 | tf_op jit(solution)/shard_map/all_gather | solution.py:170
  180.5 16.6 %reduce-scatter.43.cloned.1.call-done = bf16[1,256,768]{2,1,0:T(8,128)(2,1)} async-done(((bf16[1,512,768]{2,1,0:T(8,128)(2,1)}), bf16[1,256,768]{2,1,0:T(8,128)(2,1)}) %reduce-scatter.43.cloned.1.call-update) | async-done | bytes 393232 | tf_op jit(solution)/shard_map/reduce_scatter | solution.py:206
  205.5 9.3 collective-permute-done.3
  262.0 20.3 %all_gather.46 = bf16[1,512,768]{2,1,0:T(8,128)(2,1)} all-gather(bf16[1,256,768]{2,1,0:T(8,128)(2,1)} %get-tuple-element.113), channel_id=1, replica_groups=mesh['dp'=16,'mp'=2] {'mp'}, dimensions={1}, use_global_device_ids=true | all-gather | bytes 1179648 | tf_op jit(solution)/shard_map/all_gather | solution.py:154
  282.3 18.2 %all_gather.42 = bf16[1,512,768]{2,1,0:T(8,128)(2,1)} all-gather(bf16[1,256,768]{2,1,0:T(8,128)(2,1)} %get-tuple-element.112), channel_id=1, replica_groups=mesh['dp'=16,'mp'=2] {'mp'}, dimensions={1}, use_global_device_ids=true | all-gather | bytes 1179648 | tf_op jit(solution)/shard_map/all_gather | solution.py:154
  300.5 8.5 all_gather.40
  309.1 19.4 %reduce-scatter.17.cloned.1.call-done = f32[1,256,768]{2,1,0:T(8,128)} async-done(((f32[1,512,768]{2,1,0:T(8,128)}), f32[1,256,768]{2,1,0:T(8,128)}) %reduce-scatter.17.cloned.1.call-update) | async-done | bytes 786448 | tf_op jit(solution)/shard_map/reduce_scatter | solution.py:139
  332.1 11.6 %all_gather.39 = bf16[1,512,768]{2,1,0:T(8,128)(2,1)} all-gather(bf16[1,256,768]{2,1,0:T(8,128)(2,1)S(1)} %get-tuple-element.121), channel_id=1, replica_groups=mesh['dp'=16,'mp'=2] {'mp'}, dimensions={1}, use_global_device_ids=true | all-gather | bytes 1179648 | tf_op jit(solution)/shard_map/all_gather | solution.py:144
  343.7 10.6 %all_gather.37 = bf16[1,512,768]{2,1,0:T(8,128)(2,1)S(1)} all-gather(bf16[1,256,768]{2,1,0:T(8,128)(2,1)S(1)} %get-tuple-element.120), channel_id=1, replica_groups=mesh['dp'=16,'mp'=2] {'mp'}, dimensions={1}, use_global_device_ids=true | all-gather | bytes 1179648 | tf_op jit(solution)/shard_map/all_gather | solution.py:144
  354.4 9.4 %fusion.13 = (bf16[512,1536]{1,0:T(8,128)(2,1)}, f32[512,1536]{1,0:T(8,128)S(1)}) fusion(f32[1536]{0:T(1024)S(1)} %copy-done.192, bf16[768,1536]{1,0:T(8,128)(2,1)S(1)} %copy-done, bf16[1,512,768]{2,1,0:T(8,128)(2,1)S(1)} %all_gather.37), kind=kOutput, calls=%fused_computation.51 | convolution fusion | flops 1259864064 | bytes 7870464 | tf_op jit(solution)/shard_map/bsd,df->bsf/dot_general | solution.py:54
  363.8 10.0 %all_gather.36 = bf16[1,512,768]{2,1,0:T(8,128)(2,1)} all-gather(bf16[1,256,768]{2,1,0:T(8,128)(2,1)S(1)} %get-tuple-element.119), channel_id=1, replica_groups=mesh['dp'=16,'mp'=2] {'mp'}, dimensions={1}, use_global_device_ids=true | all-gather | bytes 1179648 | tf_op jit(solution)/shard_map/all_gather | solution.py:144
  380.6 9.8 %fusion.19 = (bf16[512,1536]{1,0:T(8,128)(2,1)}, f32[512,1536]{1,0:T(8,128)S(1)}) fusion(f32[1536]{0:T(1024)S(1)} %copy-done.192, bf16[768,1536]{1,0:T(8,128)(2,1)S(1)} %copy-done, bf16[1,512,768]{2,1,0:T(8,128)(2,1)} %all_gather.39), kind=kOutput, calls=%fused_computation.57 | convolution fusion | flops 1259864064 | bytes 7870464 | tf_op jit(solution)/shard_map/bsd,df->bsf/dot_general | solution.py:54
  397.5 9.8 %fusion.10 = (bf16[512,1536]{1,0:T(8,128)(2,1)}, f32[512,1536]{1,0:T(8,128)S(1)}) fusion(f32[1536]{0:T(1024)S(1)} %copy-done.192, bf16[768,1536]{1,0:T(8,128)(2,1)S(1)} %copy-done, bf16[1,512,768]{2,1,0:T(8,128)(2,1)} %all_gather.36), kind=kOutput, calls=%fused_computation.48 | convolution fusion | flops 1259864064 | bytes 7870464 | tf_op jit(solution)/shard_map/bsd,df->bsf/dot_general | solution.py:54
  419.0 5.4 fusion.178
  434.1 5.5 fusion.197
  449.1 9.7 %add_add_fusion = f32[1536,768]{1,0:T(8,128)} fusion(f32[1536,768]{1,0:T(8,128)} %fusion.178, f32[1536,768]{1,0:T(8,128)} %fusion.189, f32[1536,768]{1,0:T(8,128)} %fusion.183, bf16[512,1536]{1,0:T(8,128)(2,1)} %get-tuple-element.146, bf16[1,512,768]{2,1,0:T(8,128)(2,1)} %all_gather.46), kind=kOutput, calls=%fused_computation.32 | convolution fusion | flops 1211498496 | bytes 21233664 | tf_op jit(solution)/shard_map/bsf,bsd->fd/dot_general | solution.py:54
  458.8 9.1 add_add_fusion.1
  471.7 12.0 %reduce-scatter.19.cloned.1.call-done = bf16[1,256,768]{2,1,0:T(8,128)(2,1)} async-done(((bf16[1,512,768]{2,1,0:T(8,128)(2,1)}), bf16[1,256,768]{2,1,0:T(8,128)(2,1)}) %reduce-scatter.19.cloned.1.call-update) | async-done | bytes 393232 | tf_op jit(solution)/shard_map/reduce_scatter | solution.py:147
  483.7 20.2 %reduce-scatter.31.cloned.1.call-done = bf16[1,256,768]{2,1,0:T(8,128)(2,1)} async-done(((bf16[1,512,768]{2,1,0:T(8,128)(2,1)}), bf16[1,256,768]{2,1,0:T(8,128)(2,1)}) %reduce-scatter.31.cloned.1.call-update) | async-done | bytes 393232 | tf_op jit(solution)/shard_map/reduce_scatter | solution.py:147
  509.5 19.6 %all_gather.41 = bf16[1,512,768]{2,1,0:T(8,128)(2,1)S(1)} all-gather(bf16[1,256,768]{2,1,0:T(8,128)(2,1)S(1)} %convert_element_type.586), channel_id=1, replica_groups=mesh['dp'=16,'mp'=2] {'mp'}, dimensions={1}, use_global_device_ids=true | all-gather | bytes 1179648 | tf_op jit(solution)/shard_map/all_gather | solution.py:170
  540.1 8.5 all_gather.43
  568.5 8.9 all_gather.47
  641.2 60.3 %all-reduce.1 = (f32[384]{0:T(512)}, f32[384]{0:T(512)}, f32[1536]{0:T(1024)}) all-reduce(f32[384]{0:T(512)} %add.708, f32[384]{0:T(512)} %add.718, f32[1536]{0:T(1024)S(1)} %add_add_fusion.2), channel_id=1, replica_groups=mesh['dp'=16,'mp'=2] {'dp'}, use_global_device_ids=true, to_apply=%region_75.77 | all-reduce | flops 2304 | bytes 18432 | tf_op jit(solution)/shard_map/psum | solution.py:213
  712.2 39.3 %all-reduce = (f32[768]{0:T(1024)}, f32[768]{0:T(1024)}, f32[768]{0:T(1024)}, f32[768]{0:T(1024)}, f32[768]{0:T(1024)}, /*index=5*/f32[768]{0:T(1024)}) all-reduce(f32[768]{0:T(1024)} %add_add_fusion.10, f32[768]{0:T(1024)} %add_add_fusion.9, f32[768]{0:T(1024)} %add_add_fusion.6, ...), channel_id=1, replica_groups=mesh['dp'=16,'mp'=2] {'dp','mp'}, use_global_device_ids=true, to_apply=%region_64.66 | all-reduce | flops 4608 | bytes 36864 | tf_op jit(solution)/shard_map/psum | solution.py:228
  761.7 152.7 %all-reduce.5.cloned.1.call-done = (f32[768,384]{1,0:T(8,128)}, f32[768,384]{1,0:T(8,128)}, f32[768,384]{1,0:T(8,128)}, f32[384,768]{1,0:T(8,128)}, f32[768,1536]{1,0:T(8,128)}, /*index=5*/f32[1536,768]{1,0:T(8,128)}) async-done(((f32[768,384]{1,0:T(8,128)}, f32[768,384]{1,0:T(8,128)}, f32[768,384]{1,0:T(8,128)}, f32[384,768]{1,0:T(8,128)}, f32[768,1536]{1,0:T(8,128)}, /*index=5*/f32[1536,768]{1,0:T(8,128)}), ...) | async-done | bytes 14155792 | tf_op jit(solution)/shard_map/psum | solution.py:213
  (672 shorter events, 299.8 us)
Async XLA Ops:
  7.2 77.9 %copy-start = (bf16[768,1536]{1,0:T(8,128)(2,1)S(1)}, bf16[768,1536]{1,0:T(8,128)(2,1)}, u32[]{:S(2)}) copy-start(bf16[768,1536]{1,0:T(8,128)(2,1)} %param.34) | copy-start | bytes 7077892
  7.2 63.3 %reduce-scatter.25.cloned.1.call-start = ((), (), s32[]{:S(2)}) async-start(), calls=%async_computation.20 | async-start | bytes 2359296 | tf_op jit(solution)/shard_map/reduce_scatter | solution.py:139
  12.9 12.4 %collective-permute-start.2 = (bf16[1,256,768]{2,1,0:T(8,128)(2,1)}, bf16[1,256,768]{2,1,0:T(8,128)(2,1)}, u32[]{:S(2)}, u32[]{:S(2)}) collective-permute-start(bf16[1,256,768]{2,1,0:T(8,128)(2,1)} %fusion.127), channel_id=1, source_target_pairs={{0,1},{1,0},{2,3},{3,2},{4,5},{5,4},{6,7},{7,6},{8,9},{9,8},{10,11... | collective-permute-start | bytes 1179656 | tf_op jit(solution)/shard_map/ppermute | solution.py:22
  39.0 90.3 %reduce-scatter.41.cloned.1.call-start = ((), (), s32[]{:S(2)}) async-start(), calls=%async_computation.28 | async-start | bytes 2359296 | tf_op jit(solution)/shard_map/reduce_scatter | solution.py:163
  101.9 47.7 %reduce-scatter.27.cloned.1.call-start = ((), (), s32[]{:S(2)}) async-start(), calls=%async_computation.21 | async-start | bytes 1179648 | tf_op jit(solution)/shard_map/reduce_scatter | solution.py:147
  106.4 90.8 %reduce-scatter.43.cloned.1.call-start = ((), (), s32[]{:S(2)}) async-start(), calls=%async_computation.29 | async-start | bytes 1179648 | tf_op jit(solution)/shard_map/reduce_scatter | solution.py:206
  179.6 129.5 %reduce-scatter.29.cloned.1.call-start = ((), (), s32[]{:S(2)}) async-start(), calls=%async_computation.22 | async-start | bytes 2359296 | tf_op jit(solution)/shard_map/reduce_scatter | solution.py:139
  202.8 12.0 %collective-permute-start.3 = (bf16[1,256,768]{2,1,0:T(8,128)(2,1)S(1)}, bf16[1,256,768]{2,1,0:T(8,128)(2,1)S(1)}, u32[]{:S(2)}, u32[]{:S(2)}) collective-permute-start(bf16[1,256,768]{2,1,0:T(8,128)(2,1)S(1)} %get-tuple-element.98), channel_id=1, source_target_pairs={{0,1},{1,0},{2,3},{3,2},{4,5},{5,4},{6,7},{7,6},{8,9},{9,8},{10,11... | collective-permute-start | bytes 1179656 | tf_op jit(solution)/shard_map/ppermute | solution.py:22
  203.7 27.4 %collective-permute-start.1 = (bf16[1,256,768]{2,1,0:T(8,128)(2,1)}, bf16[1,256,768]{2,1,0:T(8,128)(2,1)}, u32[]{:S(2)}, u32[]{:S(2)}) collective-permute-start(bf16[1,256,768]{2,1,0:T(8,128)(2,1)} %get-tuple-element.97), channel_id=1, source_target_pairs={{0,1},{1,0},{2,3},{3,2},{4,5},{5,4},{6,7},{7,6},{8,9},{9,8},{10,11... | collective-permute-start | bytes 1179656 | tf_op jit(solution)/shard_map/ppermute | solution.py:22
  229.6 79.5 %reduce-scatter.21.cloned.1.call-start = ((), (), s32[]{:S(2)}) async-start(), calls=%async_computation.18 | async-start | bytes 2359296 | tf_op jit(solution)/shard_map/reduce_scatter | solution.py:139
  230.7 16.3 %collective-permute-start = (bf16[1,256,768]{2,1,0:T(8,128)(2,1)}, bf16[1,256,768]{2,1,0:T(8,128)(2,1)}, u32[]{:S(2)}, u32[]{:S(2)}) collective-permute-start(bf16[1,256,768]{2,1,0:T(8,128)(2,1)} %get-tuple-element.96), channel_id=1, source_target_pairs={{0,1},{1,0},{2,3},{3,2},{4,5},{5,4},{6,7},{7,6},{8,9},{9,8},{10,11... | collective-permute-start | bytes 1179656 | tf_op jit(solution)/shard_map/ppermute | solution.py:22
  246.1 82.4 %reduce-scatter.17.cloned.1.call-start = ((), (), s32[]{:S(2)}) async-start(), calls=%async_computation.16 | async-start | bytes 2359296 | tf_op jit(solution)/shard_map/reduce_scatter | solution.py:139
  261.9 66.5 %copy-start.169 = (f32[768]{0:T(1024)S(1)}, f32[768]{0:T(1024)}, u32[]{:S(2)}) copy-start(f32[768]{0:T(1024)} %param.31) | copy-start | bytes 9220
  262.0 206.0 %reduce-scatter.37.cloned.1.call-start = ((), (), s32[]{:S(2)}) async-start(), calls=%async_computation.26 | async-start | bytes 2359296 | tf_op jit(solution)/shard_map/reduce_scatter | solution.py:163
  331.1 136.9 %copy-start.149 = (f32[256]{0:T(256)}, f32[256]{0:T(256)S(1)}, u32[]{:S(2)}) copy-start(f32[256]{0:T(256)S(1)} %broadcast_multiply_fusion.20) | copy-start | bytes 3076
  331.3 136.6 %copy-start.175 = (f32[256]{0:T(256)}, f32[256]{0:T(256)S(1)}, u32[]{:S(2)}) copy-start(f32[256]{0:T(256)S(1)} %add_rsqrt_fusion.4) | copy-start | bytes 3076
  380.5 87.4 %reduce-scatter.45.cloned.1.call-start = ((), (), s32[]{:S(2)}) async-start(), calls=%async_computation.30 | async-start | bytes 2359296 | tf_op jit(solution)/shard_map/reduce_scatter | solution.py:163
  397.0 70.9 %reduce-scatter.33.cloned.1.call-start = ((), (), s32[]{:S(2)}) async-start(), calls=%async_computation.24 | async-start | bytes 2359296 | tf_op jit(solution)/shard_map/reduce_scatter | solution.py:163
  413.9 69.8 %reduce-scatter.19.cloned.1.call-start = ((), (), s32[]{:S(2)}) async-start(), calls=%async_computation.17 | async-start | bytes 1179648 | tf_op jit(solution)/shard_map/reduce_scatter | solution.py:147
  418.9 85.0 %reduce-scatter.31.cloned.1.call-start = ((), (), s32[]{:S(2)}) async-start(), calls=%async_computation.23 | async-start | bytes 1179648 | tf_op jit(solution)/shard_map/reduce_scatter | solution.py:147
  433.8 103.0 %reduce-scatter.23.cloned.1.call-start = ((), (), s32[]{:S(2)}) async-start(), calls=%async_computation.19 | async-start | bytes 1179648 | tf_op jit(solution)/shard_map/reduce_scatter | solution.py:147
  449.0 256.8 %reduce-scatter.35.cloned.1.call-start = ((), (), s32[]{:S(2)}) async-start(), calls=%async_computation.25 | async-start | bytes 1179648 | tf_op jit(solution)/shard_map/reduce_scatter | solution.py:206
  589.0 116.8 %reduce-scatter.39.cloned.1.call-start = ((), (), s32[]{:S(2)}) async-start(), calls=%async_computation.27 | async-start | bytes 1179648 | tf_op jit(solution)/shard_map/reduce_scatter | solution.py:206
  607.8 98.0 %reduce-scatter.47.cloned.1.call-start = ((), (), s32[]{:S(2)}) async-start(), calls=%async_computation.31 | async-start | bytes 1179648 | tf_op jit(solution)/shard_map/reduce_scatter | solution.py:206
  622.3 292.1 %all-reduce.5.cloned.1.call-start = ((), (), s32[]{:S(2)}) async-start(), calls=%async_computation.32 | async-start | bytes 28311552 | tf_op jit(solution)/shard_map/psum | solution.py:213
  630.6 70.9 %copy-start.108 = (bf16[1,256,768]{2,1,0:T(8,128)(2,1)S(1)}, bf16[1,256,768]{2,1,0:T(8,128)(2,1)}, u32[]{:S(2)}) copy-start(bf16[1,256,768]{2,1,0:T(8,128)(2,1)} %get-tuple-element.115) | copy-start | bytes 1179652
  630.6 70.9 %copy-start.115 = (bf16[1,256,768]{2,1,0:T(8,128)(2,1)S(1)}, bf16[1,256,768]{2,1,0:T(8,128)(2,1)}, u32[]{:S(2)}) copy-start(bf16[1,256,768]{2,1,0:T(8,128)(2,1)} %get-tuple-element.118) | copy-start | bytes 1179652
  630.6 70.9 %copy-start.119 = (bf16[1,256,768]{2,1,0:T(8,128)(2,1)S(1)}, bf16[1,256,768]{2,1,0:T(8,128)(2,1)}, u32[]{:S(2)}) copy-start(bf16[1,256,768]{2,1,0:T(8,128)(2,1)} %get-tuple-element.116) | copy-start | bytes 1179652
  630.6 75.2 %copy-start.143 = (f32[768]{0:T(1024)S(1)}, f32[768]{0:T(1024)}, u32[]{:S(2)}) copy-start(f32[768]{0:T(1024)} %param.23) | copy-start | bytes 9220
  630.6 75.2 %copy-start.148 = (f32[256]{0:T(256)S(1)}, f32[256]{0:T(256)}, u32[]{:S(2)}) copy-start(f32[256]{0:T(256)} %copy-done.147) | copy-start | bytes 3076
  705.8 52.6 %copy-start.46 = (f32[1,256,768]{2,1,0:T(8,128)S(1)}, f32[1,256,768]{2,1,0:T(8,128)}, u32[]{:S(2)}) copy-start(f32[1,256,768]{2,1,0:T(8,128)} %copy-done.45) | copy-start | bytes 2359300
  705.8 52.6 %copy-start.153 = (f32[256]{0:T(256)S(1)}, f32[256]{0:T(256)}, u32[]{:S(2)}) copy-start(f32[256]{0:T(256)} %copy-done.152) | copy-start | bytes 3076
  (203 other events, 1416.7 us)
Sparse Core Ops, SparseCore 0:
  39.1 31.3 reduce-scatter.24
  102.0 27.2 reduce-scatter.40
  132.1 17.4 reduce-scatter.26
  179.7 17.4 reduce-scatter.42
  229.7 28.2 reduce-scatter.28
  260.7 38.1 reduce-scatter.20
  301.7 26.6 reduce-scatter.16
  380.6 26.0 reduce-scatter.36
  409.0 26.0 reduce-scatter.44
  437.3 26.0 reduce-scatter.32
  466.2 17.4 reduce-scatter.18
  486.5 17.4 reduce-scatter.30
  506.7 24.0 reduce-scatter.22
  589.1 17.4 reduce-scatter.34
  608.7 17.4 reduce-scatter.38
  629.0 17.4 reduce-scatter.46
  652.6 261.7 all-reduce.4
